TPU v7x, 32 devices: a whole 2x2x4 slice. The times are simulated.
32 devices in a mesh: dom: 8 (over z, x), sub: 4 (over y, core).
Axes of the slice: x: 2, y: 2, z: 4, core: 2. Of those that a mesh axis runs over, the one named last changes fastest.
Arguments:
- positions: float32 [3, 1048576], P(None, ('dom', 'sub')), may hold values from -0.11 to 1.11
- velocities: float32 [3, 1048576], P(None, ('dom', 'sub')), may hold values from -3 to 3
- masses: float32 [1048576], P(('dom', 'sub')), may hold values from 0.003 to 0.012
- accel_prev: float32 [3, 1048576], P(None, ('dom', 'sub')), may hold values from -180 to 180
- active: int32 [1048576], P(('dom', 'sub')), may hold values from 0 to 1, as said below
- bucket_top: int32 [4096], P(('dom', 'sub')), may hold values from 0 to 4095
- near_list: int32 [4096, 4], P(('dom', 'sub')), may hold values from 0 to 511, as said below
- cell_list: int32 [4096, 64], P(('dom', 'sub')), may hold values from 0 to 1023
- top_list: int32 [4096, 32], P(('dom', 'sub')), may hold values from 0 to 4095
- essential: int32 [8, 4, 8, 32], P('dom', 'sub'), may hold values from 0 to 511
- work: int32 [1280], P(('dom', 'sub')), may hold values from 0 to 511, as said below
Outputs:
- vel_out: float32 [3, 1048576], P(None, ('dom', 'sub'))
- pos_out: float32 [3, 1048576], P(None, ('dom', 'sub'))
Inputs may be any that keep to these rules, and one draw needn't show every extreme that they name: near_list[n, 0] is the group-local number of bucket n itself; every entry of row n names a bucket of n's group whose top cell differs from n's by at most one in each of the three top-cell coordinates. A bucket holds an active particle exactly when its group-local number appears in its group's block of work. `work`: entries g * 4 * 40 to (g + 1) * 4 * 40 - 1 are the block of domain group g and name distinct group-local buckets; in every group one device holds 128 of the named buckets.
All inputs are finite; a program needn't handle non-finite values.
Results may differ from a plain program's by a relative error of at most 0.0003.
Values sent between devices are 32-bit elements; how exact they have to be, the bound alone decides.
No kernel may reach another device: no remote copies, remote signals or barrier semaphores. Data moves between devices by JAX's collectives and lax.ppermute only.
A program may use at most 64 MiB of HBM per device.

v0:
```python
import jax
import jax.numpy as jnp
from jax import lax
from jax.sharding import PartitionSpec as P

TOP_SIDE = 16
STEPS = 2
TOP = 4096
time_step = 0.01
soften = 0.0025
mass_floor = 0.5


def top_centres(top_ids):
    cell_side = TOP_SIDE
    first_index = top_ids // (cell_side * cell_side)
    second_index = top_ids // cell_side % cell_side
    third_index = top_ids % cell_side
    stacked = jnp.stack([first_index, second_index, third_index]).astype(jnp.float32)
    return (stacked + 0.5) / cell_side


def bucket_moments(places, weights):
    mass_total = jnp.sum(weights, axis=1)
    centre = jnp.sum(places * weights[None], axis=2) / mass_total[None]
    offsets = places - centre[:, :, None]
    radius_sq = jnp.sum(offsets * offsets, axis=0)

    def diagonal(first_axis):
        return jnp.sum(
            weights * (3.0 * offsets[first_axis] * offsets[first_axis] - radius_sq), axis=1
        )

    def crossed(first_axis, second_axis):
        return 3.0 * jnp.sum(weights * offsets[first_axis] * offsets[second_axis], axis=1)

    quadrupole = jnp.stack(
        [diagonal(0), diagonal(1), diagonal(2), crossed(0, 1), crossed(0, 2), crossed(1, 2)]
    )
    return jnp.concatenate([mass_total[None], centre, quadrupole], axis=0)


def top_raw(places, weights, centres):
    offsets = places - centres[:, :, None]
    weighted = weights[None] * offsets
    row_list = [
        weights,
        weighted[0],
        weighted[1],
        weighted[2],
        weighted[0] * offsets[0],
        weighted[1] * offsets[1],
        weighted[2] * offsets[2],
        weighted[0] * offsets[1],
        weighted[0] * offsets[2],
        weighted[1] * offsets[2],
    ]
    return jnp.stack([jnp.sum(row_values, axis=1) for row_values in row_list])


def top_moments(raw_sums, centres):
    mass_total = raw_sums[0]
    safe_mass = jnp.maximum(mass_total, mass_floor)
    first_sums = raw_sums[1:4]
    centre = centres + first_sums / safe_mass[None]
    cov_xx = raw_sums[4] - first_sums[0] * first_sums[0] / safe_mass
    cov_yy = raw_sums[5] - first_sums[1] * first_sums[1] / safe_mass
    cov_zz = raw_sums[6] - first_sums[2] * first_sums[2] / safe_mass
    cov_xy = raw_sums[7] - first_sums[0] * first_sums[1] / safe_mass
    cov_xz = raw_sums[8] - first_sums[0] * first_sums[2] / safe_mass
    cov_yz = raw_sums[9] - first_sums[1] * first_sums[2] / safe_mass
    trace_sum = cov_xx + cov_yy + cov_zz
    quadrupole = jnp.stack(
        [
            3.0 * cov_xx - trace_sum,
            3.0 * cov_yy - trace_sum,
            3.0 * cov_zz - trace_sum,
            3.0 * cov_xy,
            3.0 * cov_xz,
            3.0 * cov_yz,
        ]
    )
    return jnp.concatenate([mass_total[None], centre, quadrupole], axis=0)


def pair_accel(targets, sources, source_mass):
    offsets = sources[:, :, None] - targets[:, None, :]
    distance = jnp.sum(offsets * offsets, axis=0) + soften
    inverse = lax.rsqrt(distance)
    strength = source_mass[:, None] * inverse * inverse * inverse
    return jnp.sum(offsets * strength[None], axis=1)


def cell_accel(targets, moments):
    offsets = targets[:, None, :] - moments[1:4, :, None]
    distance = jnp.sum(offsets * offsets, axis=0) + soften
    inverse = lax.rsqrt(distance)
    inverse_sq = inverse * inverse
    inverse_three = inverse * inverse_sq
    inverse_five = inverse_three * inverse_sq
    inverse_seven = inverse_five * inverse_sq
    quadrupole = moments[4:10, :, None]
    along_x = quadrupole[0] * offsets[0] + quadrupole[3] * offsets[1] + quadrupole[4] * offsets[2]
    along_y = quadrupole[3] * offsets[0] + quadrupole[1] * offsets[1] + quadrupole[5] * offsets[2]
    along_z = quadrupole[4] * offsets[0] + quadrupole[5] * offsets[1] + quadrupole[2] * offsets[2]
    contracted = offsets[0] * along_x + offsets[1] * along_y + offsets[2] * along_z
    radial = -moments[0][:, None] * inverse_three - 2.5 * contracted * inverse_seven
    along_all = jnp.stack([along_x, along_y, along_z])
    return jnp.sum(offsets * radial[None] + along_all * inverse_five[None], axis=1)


def force_one(
    target, near_ids, cell_ids, top_ids, group_places, group_mass, essential_cells, top_cells
):
    sources = group_places[:, near_ids].reshape(3, -1)
    source_mass = group_mass[near_ids].reshape(-1)
    moments = jnp.concatenate(
        [jnp.take(essential_cells, cell_ids, axis=1), jnp.take(top_cells, top_ids, axis=1)], axis=1
    )
    return pair_accel(target, sources, source_mass) + cell_accel(target, moments)


def in_blocks(step_function, inputs, item_count):
    block_width = 4

    def reshape_leaf(values):
        return values.reshape((item_count // block_width, block_width) + values.shape[1:])

    result = lax.map(jax.vmap(step_function), jax.tree.map(reshape_leaf, inputs))
    return result.reshape((item_count,) + result.shape[2:])


def body(
    positions,
    velocities,
    masses,
    accel_prev,
    active,
    bucket_top,
    near_list,
    cell_list,
    top_list,
    essential,
    work,
):
    bucket_count = bucket_top.shape[0]
    bucket_size = positions.shape[1] // bucket_count
    sub_count = lax.axis_size("sub")
    dom_count = lax.axis_size("dom")
    sub_index = lax.axis_index("sub")
    group_buckets = sub_count * bucket_count
    activity = active.astype(jnp.float32)
    bucket_centres = top_centres(bucket_top)
    all_top_ids = jnp.arange(TOP, dtype=jnp.int32)
    placement = (bucket_top[:, None] == all_top_ids[None, :]).astype(jnp.float32)
    incoming = lax.all_to_all(
        essential.reshape(dom_count, -1), "dom", split_axis=0, concat_axis=0, tiled=True
    ).reshape(-1)
    shared_near, shared_cells, shared_tops, shared_work = (
        lax.all_gather(near_list, "sub", axis=0, tiled=True),
        lax.all_gather(cell_list, "sub", axis=0, tiled=True),
        lax.all_gather(top_list, "sub", axis=0, tiled=True),
        lax.all_gather(work, "sub", axis=0, tiled=True),
    )
    work_near = shared_near[work]
    work_cells = shared_cells[work]
    work_tops = shared_tops[work]
    own_ids = sub_index * bucket_count + jnp.arange(bucket_count, dtype=jnp.int32)
    matches = (own_ids[:, None] == shared_work[None, :]).astype(jnp.float32)
    places = positions
    speeds = velocities
    accel_now = accel_prev
    for substep in range(STEPS):
        half_speed = speeds + 0.5 * time_step * activity * accel_now
        places = places + time_step * half_speed
        group_places, group_mass = (
            lax.all_gather(places, "sub", axis=1, tiled=True),
            lax.all_gather(masses, "sub", axis=0, tiled=True),
        )
        group_places = group_places.reshape(3, group_buckets, bucket_size)
        group_mass = group_mass.reshape(group_buckets, bucket_size)
        group_cells = bucket_moments(group_places, group_mass)
        replies = lax.all_to_all(
            jnp.take(group_cells, incoming, axis=1), "dom", split_axis=1, concat_axis=1, tiled=True
        )
        essential_cells = lax.all_gather(replies, "sub", axis=1, tiled=True)
        own_places = places.reshape(3, bucket_count, bucket_size)
        own_mass = masses.reshape(bucket_count, bucket_size)
        spread_sums = jnp.dot(
            top_raw(own_places, own_mass, bucket_centres),
            placement,
            precision=lax.Precision.HIGHEST,
        )
        totals = lax.psum(spread_sums, ("dom", "sub"))
        top_cells = top_moments(totals, top_centres(all_top_ids))

        def one_bucket(work_item):
            target, near_ids, cell_ids, top_ids = work_item
            return force_one(
                target,
                near_ids,
                cell_ids,
                top_ids,
                group_places,
                group_mass,
                essential_cells,
                top_cells,
            )

        targets = jnp.transpose(group_places[:, work], (1, 0, 2))
        forces = in_blocks(one_bucket, (targets, work_near, work_cells, work_tops), work.shape[0])
        returned = lax.all_gather(forces, "sub", axis=0, tiled=True)
        accel_own = jnp.einsum("bw,wcp->cbp", matches, returned, precision=lax.Precision.HIGHEST)
        accel_now = accel_own.reshape(3, -1)
        speeds = half_speed + 0.5 * time_step * activity * accel_now
    return (speeds, places)


def solution(mesh):
    in_specs = (
        P(None, ("dom", "sub")),
        P(None, ("dom", "sub")),
        P(("dom", "sub")),
        P(None, ("dom", "sub")),
        P(("dom", "sub")),
        P(("dom", "sub")),
        P(("dom", "sub"), None),
        P(("dom", "sub"), None),
        P(("dom", "sub"), None),
        P("dom", "sub", None, None),
        P(("dom", "sub")),
    )
    out_specs = (P(None, ("dom", "sub")), P(None, ("dom", "sub")))
    return jax.shard_map(body, mesh=mesh, in_specs=in_specs, out_specs=out_specs, check_vma=False)
```

profile of v0, /device:TPU:0, one launch (start us, length us, event | category | flops | bytes accessed | tf_op | source)
XLA Modules:
  0.0 734.8 jit_solution(12766479794120827817)
XLA Ops:
  15.1 7.3 all-to-all-start
  22.4 7.3 all_gather.36
  30.0 7.7 %all_gather.37 = s32[512,64]{1,0:T(8,128)S(1)} all-gather(s32[128,64]{1,0:T(8,128)S(1)} %copy.152), channel_id=1, replica_groups=mesh['dom'=8,'sub'=4] {'sub'}, dimensions={0}, use_global_device_ids=true | all-gather | bytes 163840 | tf_op jit(solution)/shard_map/all_gather | solution.py:161
  37.9 6.9 all_gather.39
  45.3 5.8 all_gather.34
  55.8 4.8 all-reduce
  62.0 91.1 %all-reduce.4.cloned.1.call-done = f32[10,4096]{1,0:T(8,128)} async-done(((f32[10,4096]{1,0:T(8,128)}), f32[10,4096]{1,0:T(8,128)}) %all-reduce.4.cloned.1.call-update) | async-done | bytes 163856 | tf_op jit(solution)/shard_map/psum | solution.py:194
  158.9 2.3 fusion.91
  161.9 2.6 multiply_reduce_fusion.3
  169.5 4.5 all-to-all-start.1
  182.1 5.4 all_gather.38
  188.4 178.6 %while.20 = (s32[]{:T(128)}, f32[10,4,3,256]{3,2,1,0:T(4,128)}, s32[10,4,4]{2,1,0:T(4,128)S(1)}, f32[3,512,256]{2,0,1:T(4,128)S(1)}, f32[10,4,3,256]{3,1,2,0:T(4...) while((s32[]{:T(128)}, f32[10,4,3,256]{3,2,1,0:T(4,128)}, ...), condition=%wide.region_25.29_spmd, body=%wide.region_20.28_spmd.sunk | while | flops 29599920 | bytes 26094408 | solution.py:129
  189.8 4.1 fusion.112
  194.5 2.7 multiply_multiply_fusion.18
  200.0 2.2 gather_fusion.2
  207.7 4.1 fusion.112
  212.4 2.7 multiply_multiply_fusion.18
  217.8 2.2 gather_fusion.2
  225.5 4.1 fusion.112
  230.3 2.7 multiply_multiply_fusion.18
  243.4 4.1 fusion.112
  248.1 2.7 multiply_multiply_fusion.18
  261.2 4.1 fusion.112
  266.0 2.7 multiply_multiply_fusion.18
  279.1 4.1 fusion.112
  283.8 2.7 multiply_multiply_fusion.18
  296.9 4.1 fusion.112
  301.7 2.7 multiply_multiply_fusion.18
  314.8 4.1 fusion.112
  319.5 2.7 multiply_multiply_fusion.18
  332.7 4.1 fusion.112
  337.4 2.7 multiply_multiply_fusion.18
  350.5 4.1 fusion.112
  355.2 2.7 multiply_multiply_fusion.18
  368.0 7.1 all_gather.40
  381.0 129.9 %all-reduce.6.cloned.1.call-done = f32[10,4096]{1,0:T(8,128)} async-done(((f32[10,4096]{1,0:T(8,128)}), f32[10,4096]{1,0:T(8,128)}) %all-reduce.6.cloned.1.call-update) | async-done | bytes 163856 | tf_op jit(solution)/shard_map/psum | solution.py:194
  519.6 2.5 multiply_reduce_fusion.2
  527.3 4.5 all-to-all-start.2
  535.5 2.9 all-to-all-done.2
  539.3 5.2 all_gather.43
  544.8 172.8 %while.21 = (s32[]{:T(128)}, f32[10,4,3,256]{3,2,1,0:T(4,128)S(1)}, s32[10,4,4]{2,1,0:T(4,128)S(1)}, f32[3,512,256]{2,0,1:T(4,128)S(1)}, f32[10,4,3,256]{3,1,2,0...) while((s32[]{:T(128)}, f32[10,4,3,256]{3,2,1,0:T(4,128)S(1)}, ...), condition=%wide.region_49.53_spmd, body=%wide.region_44.52_spmd.sunk | while | flops 29599920 | bytes 26098504 | solution.py:129
  546.2 4.1 fusion.120
  550.9 2.7 multiply_multiply_fusion.20
  556.4 2.2 gather_fusion.6
  563.5 4.1 fusion.120
  568.2 2.7 multiply_multiply_fusion.20
  573.7 2.2 gather_fusion.6
  580.8 4.1 fusion.120
  585.5 2.7 multiply_multiply_fusion.20
  598.1 4.1 fusion.120
  602.8 2.7 multiply_multiply_fusion.20
  615.3 4.1 fusion.120
  620.1 2.7 multiply_multiply_fusion.20
  632.6 4.1 fusion.120
  637.3 2.7 multiply_multiply_fusion.20
  649.9 4.1 fusion.120
  654.6 2.7 multiply_multiply_fusion.20
  667.2 4.1 fusion.120
  671.9 2.7 multiply_multiply_fusion.20
  684.5 4.1 fusion.120
  689.2 2.7 multiply_multiply_fusion.20
  701.7 4.1 fusion.120
  706.5 2.7 multiply_multiply_fusion.20
  717.7 7.2 all_gather.44
  (796 shorter events, 266.3 us)
Async XLA Ops:
  8.0 145.0 %all-reduce.4.cloned.1.call-start = ((), (), s32[]{:S(2)}) async-start(), calls=%async_computation.4 | async-start | bytes 524288 | tf_op jit(solution)/shard_map/psum | solution.py:194
  9.0 4.0 copy-start.11
  10.8 2.2 copy-start.22
  10.8 2.2 copy-start.16
  10.8 2.2 copy-start.28
  12.4 2.2 copy-start.2
  12.5 10.0 %copy-start.14 = (f32[32768]{0:T(1024)S(1)}, f32[32768]{0:T(1024)}, u32[]{:S(2)}) copy-start(f32[32768]{0:T(1024)} %param.23) | copy-start | bytes 393220
  12.5 17.3 %copy-start.27 = (s32[128,4]{0,1:T(4,128)S(1)}, s32[128,4]{0,1:T(4,128)}, u32[]{:S(2)}) copy-start(s32[128,4]{0,1:T(4,128)} %param.27) | copy-start | bytes 6148
  12.5 17.4 %copy-start.30 = (s32[40]{0:T(128)S(1)}, s32[40]{0:T(128)}, u32[]{:S(2)}) copy-start(s32[40]{0:T(128)} %param.31) | copy-start | bytes 484
  12.5 17.4 %copy-start.15 = (s32[128,64]{0,1:T(8,128)S(1)}, s32[128,64]{0,1:T(8,128)}, u32[]{:S(2)}) copy-start(s32[128,64]{0,1:T(8,128)} %param.28) | copy-start | bytes 98308
  12.5 25.3 %copy-start.18 = (s32[128,32]{0,1:T(8,128)S(1)}, s32[128,32]{0,1:T(8,128)}, u32[]{:S(2)}) copy-start(s32[128,32]{0,1:T(8,128)} %param.29) | copy-start | bytes 49156
  14.6 141.4 %all-gather.3.cloned.1.call-start = ((), (), s32[]{:S(2)}) async-start(), calls=%async_computation.3 | async-start | bytes 2621440 | tf_op jit(solution)/shard_map/all_gather | solution.py:177
  15.1 39.2 %copy-start.31 = (u32[32]{0:T(128)S(1)}, u32[32]{0:T(128)}, u32[]{:S(2)}) copy-start(u32[32]{0:T(128)} %constant.197) | copy-start | bytes 388
  15.1 45.5 %all-to-all-start = ((s32[8,1,32]{2,1,0:T(1,128)}), s32[8,1,32]{2,1,0:T(1,128)S(1)}, u32[]{:S(2)}, u32[]{:S(2)}) async-start(s32[8,1,32]{2,1,0:T(1,128)} %bitcast.56), calls=%async_computation | async-start | bytes 8192 | tf_op jit(solution)/shard_map/all_to_all | solution.py:156
  29.9 147.3 %copy-start.19 = (s32[1024]{0:T(1024)}, s32[1024]{0:T(1024)S(1)}, u32[]{:S(2)}) copy-start(s32[1024]{0:T(1024)S(1)} %pad_clamp_fusion.7) | copy-start | bytes 12292
  61.9 105.9 %copy-start.20 = (s32[1024]{0:T(1024)}, s32[1024]{0:T(1024)S(1)}, u32[]{:S(2)}) copy-start(s32[1024]{0:T(1024)S(1)} %pad_clamp_fusion.6) | copy-start | bytes 12292
  62.0 106.6 %copy-start.25 = (pred[256]{0:T(512)(128)(4,1)}, pred[256]{0:T(512)(128)(4,1)S(1)}, u32[]{:S(2)}) copy-start(pred[256]{0:T(512)(128)(4,1)S(1)} %compare_and_fusion.4) | copy-start | bytes 772
  155.9 2.3 copy-start.1
  169.5 11.1 %all-to-all-start.1 = ((f32[8,1,320]{2,1,0:T(1,128)}), f32[8,1,320]{2,1,0:T(1,128)S(1)}, u32[]{:S(2)}, u32[]{:S(2)}) async-start(f32[8,1,320]{2,1,0:T(1,128)} %reshape.930), calls=%async_computation.1 | async-start | bytes 24576 | tf_op jit(solution)/shard_map/all_to_all | solution.py:183
  174.0 336.9 %all-reduce.6.cloned.1.call-start = ((), (), s32[]{:S(2)}) async-start(), calls=%async_computation.6 | async-start | bytes 524288 | tf_op jit(solution)/shard_map/psum | solution.py:194
  367.0 11.0 %copy-start.3 = (f32[3,32768]{1,0:T(4,128)S(1)}, f32[3,32768]{1,0:T(4,128)}, u32[]{:S(2)}) copy-start(f32[3,32768]{1,0:T(4,128)} %copy-done.2) | copy-start | bytes 1179652
  367.0 11.0 %copy-start.4 = (f32[3,32768]{1,0:T(4,128)S(1)}, f32[3,32768]{1,0:T(4,128)}, u32[]{:S(2)}) copy-start(f32[3,32768]{1,0:T(4,128)} %param.22) | copy-start | bytes 1179652
  367.0 11.0 %copy-start.6 = (f32[3,32768]{1,0:T(4,128)S(1)}, f32[3,32768]{1,0:T(4,128)}, u32[]{:S(2)}) copy-start(f32[3,32768]{1,0:T(4,128)} %param.24) | copy-start | bytes 1179652
  367.0 11.0 %copy-start.12 = (f32[32768]{0:T(1024)S(1)}, f32[32768]{0:T(1024)}, u32[]{:S(2)}) copy-start(f32[32768]{0:T(1024)} %copy-done.11) | copy-start | bytes 393220
  376.7 1.7 copy-start.17
  377.2 0.8 copy-start.9
  378.0 0.8 copy-start.23
  378.0 0.9 copy-start.29
  378.4 2.3 copy-start.8
  380.4 134.3 %all-gather.5.cloned.1.call-start = ((), (), s32[]{:S(2)}) async-start(), calls=%async_computation.5 | async-start | bytes 2621440 | tf_op jit(solution)/shard_map/all_gather | solution.py:177
  514.8 2.2 copy-start
  522.1 4.2 copy-start.26
  527.3 11.1 %all-to-all-start.2 = ((f32[8,1,320]{2,1,0:T(1,128)}), f32[8,1,320]{2,1,0:T(1,128)S(1)}, u32[]{:S(2)}, u32[]{:S(2)}) async-start(f32[8,1,320]{2,1,0:T(1,128)} %reshape.932), calls=%async_computation.2 | async-start | bytes 24576 | tf_op jit(solution)/shard_map/all_to_all | solution.py:183
  544.8 180.1 %copy-start.21 = (s32[160]{0:T(256)S(1)}, s32[160]{0:T(256)}, u32[]{:S(2)}) copy-start(s32[160]{0:T(256)} %all-reduce) | copy-start | bytes 1924
  544.8 180.1 %copy-start.24 = (s32[128]{0:T(128)S(1)}, s32[128]{0:T(128)}, u32[]{:S(2)}) copy-start(s32[128]{0:T(128)} %iota_add_fusion) | copy-start | bytes 1540
  717.6 8.7 %copy-start.5 = (f32[3,32768]{1,0:T(4,128)S(1)}, f32[3,32768]{1,0:T(4,128)}, u32[]{:S(2)}) copy-start(f32[3,32768]{1,0:T(4,128)} %param.22) | copy-start | bytes 1179652
  717.6 8.7 %copy-start.7 = (f32[3,32768]{1,0:T(4,128)S(1)}, f32[3,32768]{1,0:T(4,128)}, u32[]{:S(2)}) copy-start(f32[3,32768]{1,0:T(4,128)} %param.24) | copy-start | bytes 1179652
  717.6 8.7 %copy-start.10 = (f32[1,3,128,256]{3,1,2,0:T(4,128)S(1)}, f32[1,3,128,256]{3,1,2,0:T(4,128)}, u32[]{:S(2)}) copy-start(f32[1,3,128,256]{3,1,2,0:T(4,128)} %copy-done.9) | copy-start | bytes 1179652
  717.6 8.7 %copy-start.13 = (f32[32768]{0:T(1024)S(1)}, f32[32768]{0:T(1024)}, u32[]{:S(2)}) copy-start(f32[32768]{0:T(1024)} %copy-done.11) | copy-start | bytes 393220
Sparse Core Ops, SparseCore 0:
  14.9 138.1 all-reduce.3
  380.5 130.3 all-reduce.5
Sparse Core Ops, SparseCore 1:
  17.2 27.6 all-gather.2
  383.0 21.0 all-gather.4
where the time goes:
time: 738 us; the launch traced here: 735 us
  other arithmetic  275 us (37%)
  waiting for transfers between devices  227 us (31%)
  local copies, waits for them, and re-layouts  135 us (18%)
  blocking collectives  57.5 us (8%)
  between operations  16.9 us (2%)
  starting transfers between devices  16.8 us (2%)
    psum x2, waiting for transfers between devices, body(): totals = lax.psum(spread_sums, ('dom', 'sub'))  221 us
    reduce_sum x20, other arithmetic, pair_accel(): distance = jnp.sum(offsets * offsets, axis=0) + soften  82.5 us
    mul x20, other arithmetic, pair_accel(): strength = source_mass[:, None] * inverse * inverse * inverse  53.3 us
    gather x40, local copies, waits for them, and re-layouts, force_one(): jnp.take(top_cells, top_ids, axis=1)  46.6 us
    reduce_sum x20, other arithmetic, pair_accel(): return jnp.sum(offsets * strength[None], axis=1)  39.3 us
    gather x40, local copies, waits for them, and re-layouts, force_one(): jnp.take(essential_cells, cell_ids, axis=1)  16.5 us
  transfers between devices with their start and end apart: 7, of which 4 were waited for; matrix products, arithmetic and copies ran while one was open for 3% of the time, Pallas kernels for 0%

commit v1 on v0

--- a/solution.py
+++ b/solution.py
@@ -191,7 +191,8 @@
             placement,
             precision=lax.Precision.HIGHEST,
         )
-        totals = lax.psum(spread_sums, ("dom", "sub"))
+        parts = lax.all_gather(spread_sums, ("dom", "sub"), axis=0, tiled=False)
+        totals = parts.sum(axis=0)
         top_cells = top_moments(totals, top_centres(all_top_ids))
 
         def one_bucket(work_item):

time: 738 us -> 626 us (0.85)
  waiting for transfers between devices: 227 us -> 97.7 us
  other arithmetic: 275 us -> 285 us
    psum x2 -> x0, waiting for transfers between devices: 221 us -> none  [body(): totals = lax.psum(spread_sums, ('dom', 'sub'))]
    all_gather x0 -> x2, waiting for transfers between devices: none -> 74.6 us  [body(): parts = lax.all_gather(spread_sums, ('dom', 'sub'), axis=0, tiled=False)]
    all_gather x2, waiting for transfers between devices: 0.05 us -> 18 us  [body(): lax.all_gather(places, 'sub', axis=1, tiled=True)]
    reduce_sum x0 -> x2, other arithmetic: none -> 8.53 us  [body(): totals = parts.sum(axis=0)]
  transfers between devices with their start and end apart: 7 -> 7, of which waited for: 4 -> 4; matrix products, arithmetic and copies ran while one was open for 3% -> 7% of each run, Pallas kernels for 0% -> 0%
where the time goes in v1:
time: 626 us; the launch traced here: 623 us
  other arithmetic  285 us (46%)
  local copies, waits for them, and re-layouts  138 us (22%)
  waiting for transfers between devices  97.7 us (16%)
  blocking collectives  61 us (10%)
  starting transfers between devices  18.7 us (3%)
  between operations  15.2 us (2%)
    reduce_sum x20, other arithmetic, pair_accel(): distance = jnp.sum(offsets * offsets, axis=0) + soften  82.5 us
    all_gather x2, waiting for transfers between devices, body(): parts = lax.all_gather(spread_sums, ('dom', 'sub'), axis=0, tiled=False)  74.6 us
    mul x20, other arithmetic, pair_accel(): strength = source_mass[:, None] * inverse * inverse * inverse  53.3 us
    gather x40, local copies, waits for them, and re-layouts, force_one(): jnp.take(top_cells, top_ids, axis=1)  46.6 us
    reduce_sum x20, other arithmetic, pair_accel(): return jnp.sum(offsets * strength[None], axis=1)  39.3 us
    all_gather x2, waiting for transfers between devices, body(): lax.all_gather(places, 'sub', axis=1, tiled=True)  18 us
    gather x40, local copies, waits for them, and re-layouts, force_one(): jnp.take(essential_cells, cell_ids, axis=1)  16.4 us
    sub x40, local copies, waits for them, and re-layouts, pair_accel(): offsets = sources[:, :, None] - targets[:, None, :]  14.4 us
  transfers between devices with their start and end apart: 7, of which 4 were waited for; matrix products, arithmetic and copies ran while one was open for 7% of the time, Pallas kernels for 0%

profile of v1, /device:TPU:0, one launch (start us, length us, event | category | flops | bytes accessed | tf_op | source)
XLA Modules:
  0.0 622.6 jit_solution(13951072991283799642)
XLA Ops:
  8.2 2.5 multiply_add_fusion.2
  14.1 7.3 %all-to-all-start = ((s32[8,1,32]{2,1,0:T(1,128)}), s32[8,1,32]{2,1,0:T(1,128)S(1)}, u32[]{:S(2)}, u32[]{:S(2)}) async-start(s32[8,1,32]{2,1,0:T(1,128)} %bitcast.56), calls=%async_computation | async-start | bytes 8192 | tf_op jit(solution)/shard_map/all_to_all | solution.py:156
  21.6 7.7 %all_gather.49 = s32[512,64]{1,0:T(8,128)S(1)} all-gather(s32[128,64]{1,0:T(8,128)S(1)} %copy.148), channel_id=1, replica_groups=mesh['dom'=8,'sub'=4] {'sub'}, dimensions={0}, use_global_device_ids=true | all-gather | bytes 163840 | tf_op jit(solution)/shard_map/all_gather | solution.py:161
  29.8 9.9 %all_gather.48 = f32[131072]{0:T(1024)S(1)} all-gather(f32[32768]{0:T(1024)S(1)} %copy-done.12), channel_id=1, replica_groups=mesh['dom'=8,'sub'=4] {'sub'}, dimensions={0}, use_global_device_ids=true | all-gather | bytes 655360 | tf_op jit(solution)/shard_map/all_gather | solution.py:178
  40.3 5.8 all_gather.46
  54.8 2.5 multiply_reduce_fusion.3
  63.7 5.5 all-to-all-start.1
  69.3 7.6 %all_gather.51 = s32[512,32]{1,0:T(8,128)S(1)} all-gather(s32[128,32]{1,0:T(8,128)} %copy.156), channel_id=1, replica_groups=mesh['dom'=8,'sub'=4] {'sub'}, dimensions={0}, use_global_device_ids=true | all-gather | bytes 81920 | tf_op jit(solution)/shard_map/all_gather | solution.py:162
  80.4 4.8 all-reduce
  88.1 5.6 all_gather.50
  93.9 26.0 %all-gather.13.cloned.1.call-done = f32[32,10,4096]{2,1,0:T(8,128)} async-done(((f32[1,10,4096]{2,1,0:T(8,128)}), f32[32,10,4096]{2,1,0:T(8,128)}) %all-gather.13.cloned.1.call-update) | async-done | bytes 5242896 | tf_op jit(solution)/shard_map/all_gather | solution.py:194
  119.9 4.6 reduce_sum.446
  129.9 2.9 copy.159
  133.5 171.9 %while.20 = (s32[]{:T(128)}, f32[10,4,3,256]{3,2,1,0:T(4,128)}, s32[10,4,4]{2,1,0:T(4,128)S(1)}, f32[3,512,256]{2,0,1:T(4,128)S(1)}, f32[10,4,3,256]{3,1,2,0:T(4...) while((s32[]{:T(128)}, f32[10,4,3,256]{3,2,1,0:T(4,128)}, ...), condition=%wide.region_25.29_spmd, body=%wide.region_20.28_spmd.sunk | while | flops 29599920 | bytes 26094908 | solution.py:129
  140.7 4.1 fusion.110
  145.5 2.7 multiply_multiply_fusion.18
  157.9 4.1 fusion.110
  162.6 2.7 multiply_multiply_fusion.18
  175.1 4.1 fusion.110
  179.8 2.7 multiply_multiply_fusion.18
  192.3 4.1 fusion.110
  197.0 2.7 multiply_multiply_fusion.18
  209.4 4.1 fusion.110
  214.2 2.7 multiply_multiply_fusion.18
  226.7 4.1 fusion.110
  231.4 2.7 multiply_multiply_fusion.18
  243.8 4.1 fusion.110
  248.5 2.7 multiply_multiply_fusion.18
  261.0 4.1 fusion.110
  265.7 2.7 multiply_multiply_fusion.18
  278.2 4.1 fusion.110
  283.0 2.7 multiply_multiply_fusion.18
  295.4 4.1 fusion.110
  300.1 2.7 multiply_multiply_fusion.18
  306.5 7.0 %all_gather.54 = f32[160,3,256]{2,0,1:T(8,128)S(1)} all-gather(f32[40,3,256]{2,0,1:T(8,128)S(1)} %copy.172), channel_id=1, replica_groups=mesh['dom'=8,'sub'=4] {'sub'}, dimensions={0}, use_global_device_ids=true | all-gather | bytes 614400 | tf_op jit(solution)/shard_map/all_gather | solution.py:213
  321.2 18.0 %all-gather.11.cloned.1.call-done = f32[3,131072]{1,0:T(4,128)} async-done(((f32[3,32768]{1,0:T(4,128)}), f32[3,131072]{1,0:T(4,128)}) %all-gather.11.cloned.1.call-update) | async-done | bytes 1572880 | tf_op jit(solution)/shard_map/all_gather | solution.py:177
  344.0 2.5 multiply_reduce_fusion.2
  351.7 5.5 all-to-all-start.2
  358.7 5.1 all-to-all-done.2
  364.7 5.5 all_gather.57
  370.4 48.6 %all-gather.15.cloned.1.call-done = f32[32,10,4096]{2,1,0:T(8,128)} async-done(((f32[1,10,4096]{2,1,0:T(8,128)}), f32[32,10,4096]{2,1,0:T(8,128)}) %all-gather.15.cloned.1.call-update) | async-done | bytes 5242896 | tf_op jit(solution)/shard_map/all_gather | solution.py:194
  419.0 3.9 reduce_sum.465
  427.4 179.0 %while.21 = (s32[]{:T(128)}, f32[10,4,3,256]{3,2,1,0:T(4,128)S(1)}, s32[10,4,4]{2,1,0:T(4,128)}, f32[3,512,256]{2,0,1:T(4,128)S(1)}, f32[10,4,3,256]{3,1,2,0:T(4...) while((s32[]{:T(128)}, f32[10,4,3,256]{3,2,1,0:T(4,128)S(1)}, ...), condition=%wide.region_49.53_spmd, body=%wide.region_44.52_spmd.sunk | while | flops 29599920 | bytes 26098496 | solution.py:129
  436.0 4.1 fusion.118
  440.7 2.7 multiply_multiply_fusion.20
  453.8 4.1 fusion.118
  458.6 2.7 multiply_multiply_fusion.20
  471.8 4.1 fusion.118
  476.5 2.7 multiply_multiply_fusion.20
  489.6 4.1 fusion.118
  494.3 2.7 multiply_multiply_fusion.20
  507.5 4.1 fusion.118
  512.2 2.7 multiply_multiply_fusion.20
  525.4 4.1 fusion.118
  530.2 2.7 multiply_multiply_fusion.20
  543.2 4.1 fusion.118
  548.0 2.7 multiply_multiply_fusion.20
  561.2 4.1 fusion.118
  565.9 2.7 multiply_multiply_fusion.20
  579.2 4.1 fusion.118
  583.9 2.7 multiply_multiply_fusion.20
  597.0 4.1 fusion.118
  601.7 2.7 multiply_multiply_fusion.20
  606.5 7.1 %all_gather.60 = f32[160,3,256]{2,0,1:T(8,128)S(1)} all-gather(f32[40,3,256]{2,0,1:T(8,128)S(1)} %copy.173), channel_id=1, replica_groups=mesh['dom'=8,'sub'=4] {'sub'}, dimensions={0}, use_global_device_ids=true | all-gather | bytes 614400 | tf_op jit(solution)/shard_map/all_gather | solution.py:213
  (814 shorter events, 273.6 us)
Async XLA Ops:
  7.2 3.6 copy-start.12
  7.2 3.7 copy-start.37
  7.2 44.7 %all-gather.9.cloned.1.call-start = ((), (), s32[]{:S(2)}) async-start(), calls=%async_computation.3 | async-start | bytes 2621440 | tf_op jit(solution)/shard_map/all_gather | solution.py:177
  8.2 4.0 copy-start.9
  10.6 10.7 %copy-start.36 = (s32[128,4]{0,1:T(4,128)S(1)}, s32[128,4]{0,1:T(4,128)}, u32[]{:S(2)}) copy-start(s32[128,4]{0,1:T(4,128)} %param.27) | copy-start | bytes 6148
  10.6 10.8 %copy-start.24 = (s32[128,64]{0,1:T(8,128)S(1)}, s32[128,64]{0,1:T(8,128)}, u32[]{:S(2)}) copy-start(s32[128,64]{0,1:T(8,128)} %param.28) | copy-start | bytes 98308
  10.7 19.1 %copy-start.39 = (s32[40]{0:T(128)S(1)}, s32[40]{0:T(128)}, u32[]{:S(2)}) copy-start(s32[40]{0:T(128)} %param.31) | copy-start | bytes 484
  10.7 109.2 %all-gather.13.cloned.1.call-start = ((), (), s32[]{:S(2)}) async-start(), calls=%async_computation.5 | async-start | bytes 8650752 | tf_op jit(solution)/shard_map/all_gather | solution.py:194
  10.9 10.4 %copy-start.31 = (f32[128]{0:T(128)}, f32[128]{0:T(128)S(1)}, u32[]{:S(2)}) copy-start(f32[128]{0:T(128)S(1)} %reduce_sum.436) | copy-start | bytes 1540
  11.0 10.4 %copy-start.25 = (f32[3,128]{1,0:T(4,128)}, f32[3,128]{1,0:T(4,128)S(1)}, u32[]{:S(2)}) copy-start(f32[3,128]{1,0:T(4,128)S(1)} %fusion.84) | copy-start | bytes 4612
  12.4 36.2 %copy-start.27 = (s32[128,32]{0,1:T(8,128)S(1)}, s32[128,32]{0,1:T(8,128)}, u32[]{:S(2)}) copy-start(s32[128,32]{0,1:T(8,128)} %param.29) | copy-start | bytes 49156
  14.1 35.5 %all-to-all-start = ((s32[8,1,32]{2,1,0:T(1,128)}), s32[8,1,32]{2,1,0:T(1,128)S(1)}, u32[]{:S(2)}, u32[]{:S(2)}) async-start(s32[8,1,32]{2,1,0:T(1,128)} %bitcast.56), calls=%async_computation | async-start | bytes 8192 | tf_op jit(solution)/shard_map/all_to_all | solution.py:156
  29.8 24.2 %copy-start.28 = (s32[1024]{0:T(1024)}, s32[1024]{0:T(1024)S(1)}, u32[]{:S(2)}) copy-start(s32[1024]{0:T(1024)S(1)} %pad_clamp_fusion.7) | copy-start | bytes 12292
  49.5 4.5 copy-start.21
  51.9 2.9 copy-start.1
  54.0 0.8 copy-start.19
  60.4 0.8 copy-start.20
  60.4 0.8 copy-start.22
  63.7 22.9 %all-to-all-start.1 = ((f32[8,1,320]{2,1,0:T(1,128)}), f32[8,1,320]{2,1,0:T(1,128)S(1)}, u32[]{:S(2)}, u32[]{:S(2)}) async-start(f32[8,1,320]{2,1,0:T(1,128)} %reshape.938), calls=%async_computation.1 | async-start | bytes 24576 | tf_op jit(solution)/shard_map/all_to_all | solution.py:183
  69.2 269.9 %all-gather.11.cloned.1.call-start = ((), (), s32[]{:S(2)}) async-start(), calls=%async_computation.4 | async-start | bytes 2621440 | tf_op jit(solution)/shard_map/all_gather | solution.py:177
  93.9 33.5 %copy-start.13 = (s32[1,4096]{1,0:T(1,128)S(1)}, s32[1,4096]{1,0:T(1,128)}, u32[]{:S(2)}) copy-start(s32[1,4096]{1,0:T(1,128)} %get-tuple-element.336) | copy-start | bytes 49156
  93.9 33.5 %copy-start.15 = (s32[1,4096]{1,0:T(1,128)S(1)}, s32[1,4096]{1,0:T(1,128)}, u32[]{:S(2)}) copy-start(s32[1,4096]{1,0:T(1,128)} %get-tuple-element.337) | copy-start | bytes 49156
  124.5 9.0 %copy-start.17 = (s32[40,4]{1,0:T(8,128)S(1)}, s32[40,4]{1,0:T(8,128)}, u32[]{:S(2)}) copy-start(s32[40,4]{1,0:T(8,128)} %gather_fusion.8) | copy-start | bytes 1924
  133.5 180.0 %copy-start.29 = (s32[160]{0:T(256)S(1)}, s32[160]{0:T(256)}, u32[]{:S(2)}) copy-start(s32[160]{0:T(256)} %all-reduce) | copy-start | bytes 1924
  133.5 180.0 %copy-start.33 = (s32[128]{0:T(128)S(1)}, s32[128]{0:T(128)}, u32[]{:S(2)}) copy-start(s32[128]{0:T(128)} %iota_add_fusion) | copy-start | bytes 1540
  305.4 12.4 %copy-start.18 = (s32[10,4,32]{2,1,0:T(4,128)}, s32[10,4,32]{2,1,0:T(4,128)S(1)}, u32[]{:S(2)}) copy-start(s32[10,4,32]{2,1,0:T(4,128)S(1)} %get-tuple-element.606) | copy-start | bytes 15364
  305.4 11.2 %copy-start.2 = (f32[3,32768]{1,0:T(4,128)S(1)}, f32[3,32768]{1,0:T(4,128)}, u32[]{:S(2)}) copy-start(f32[3,32768]{1,0:T(4,128)} %multiply_add_fusion.2) | copy-start | bytes 1179652
  305.4 11.2 %copy-start.3 = (f32[3,32768]{1,0:T(4,128)S(1)}, f32[3,32768]{1,0:T(4,128)}, u32[]{:S(2)}) copy-start(f32[3,32768]{1,0:T(4,128)} %param.22) | copy-start | bytes 1179652
  305.4 11.2 %copy-start.5 = (f32[3,32768]{1,0:T(4,128)S(1)}, f32[3,32768]{1,0:T(4,128)}, u32[]{:S(2)}) copy-start(f32[3,32768]{1,0:T(4,128)} %param.24) | copy-start | bytes 1179652
  305.4 11.2 %copy-start.10 = (f32[32768]{0:T(1024)S(1)}, f32[32768]{0:T(1024)}, u32[]{:S(2)}) copy-start(f32[32768]{0:T(1024)} %copy-done.9) | copy-start | bytes 393220
  316.3 1.8 copy-start.26
  316.6 2.7 copy-start.7
  316.6 2.9 copy-start.32
  316.7 3.0 copy-start.38
  317.8 101.2 %all-gather.15.cloned.1.call-start = ((), (), s32[]{:S(2)}) async-start(), calls=%async_computation.6 | async-start | bytes 8650752 | tf_op jit(solution)/shard_map/all_gather | solution.py:194
  319.3 22.0 %copy-start.23 = (f32[512]{0:T(512)S(1)}, f32[512]{0:T(512)}, u32[]{:S(2)}) copy-start(f32[512]{0:T(512)} %copy-done.21) | copy-start | bytes 6148
  339.1 2.2 copy-start
  346.6 4.2 copy-start.35
  351.7 12.1 %all-to-all-start.2 = ((f32[8,1,320]{2,1,0:T(1,128)}), f32[8,1,320]{2,1,0:T(1,128)S(1)}, u32[]{:S(2)}, u32[]{:S(2)}) async-start(f32[8,1,320]{2,1,0:T(1,128)} %reshape.940), calls=%async_computation.2 | async-start | bytes 24576 | tf_op jit(solution)/shard_map/all_to_all | solution.py:183
  370.4 53.9 %copy-start.14 = (s32[1,4096]{1,0:T(1,128)S(1)}, s32[1,4096]{1,0:T(1,128)}, u32[]{:S(2)}) copy-start(s32[1,4096]{1,0:T(1,128)} %get-tuple-element.336) | copy-start | bytes 49156
  370.4 53.9 %copy-start.16 = (s32[1,4096]{1,0:T(1,128)S(1)}, s32[1,4096]{1,0:T(1,128)}, u32[]{:S(2)}) copy-start(s32[1,4096]{1,0:T(1,128)} %get-tuple-element.337) | copy-start | bytes 49156
  427.4 186.2 %copy-start.30 = (s32[160]{0:T(256)S(1)}, s32[160]{0:T(256)}, u32[]{:S(2)}) copy-start(s32[160]{0:T(256)} %all-reduce) | copy-start | bytes 1924
  427.4 186.2 %copy-start.34 = (s32[128]{0:T(128)S(1)}, s32[128]{0:T(128)}, u32[]{:S(2)}) copy-start(s32[128]{0:T(128)} %iota_add_fusion) | copy-start | bytes 1540
  606.4 8.6 %copy-start.4 = (f32[3,32768]{1,0:T(4,128)S(1)}, f32[3,32768]{1,0:T(4,128)}, u32[]{:S(2)}) copy-start(f32[3,32768]{1,0:T(4,128)} %param.22) | copy-start | bytes 1179652
  606.4 8.6 %copy-start.6 = (f32[3,32768]{1,0:T(4,128)S(1)}, f32[3,32768]{1,0:T(4,128)}, u32[]{:S(2)}) copy-start(f32[3,32768]{1,0:T(4,128)} %param.24) | copy-start | bytes 1179652
  606.4 8.6 %copy-start.8 = (f32[1,3,128,256]{3,1,2,0:T(4,128)S(1)}, f32[1,3,128,256]{3,1,2,0:T(4,128)}, u32[]{:S(2)}) copy-start(f32[1,3,128,256]{3,1,2,0:T(4,128)} %copy-done.7) | copy-start | bytes 1179652
  606.4 8.6 %copy-start.11 = (f32[32768]{0:T(1024)S(1)}, f32[32768]{0:T(1024)}, u32[]{:S(2)}) copy-start(f32[32768]{0:T(1024)} %copy-done.9) | copy-start | bytes 393220
Sparse Core Ops, SparseCore 0:
  10.8 29.3 all-gather.8
  43.0 76.8 all-gather.12
  317.9 21.1 all-gather.10
  341.9 77.0 all-gather.14
